TPU v7x, 512 devices: a whole 4x8x8 slice. The times are simulated.
512 devices in a mesh: tm: 16 (over z, core), lat: 32 (over x, y).
Axes of the slice: x: 4, y: 8, z: 8, core: 2. Of those that a mesh axis runs over, the one named last changes fastest.
Arguments:
- trajectory: float32 [16, 84, 128, 128], P('tm', None, 'lat'), may hold values from -6 to 6
- step_levels: int32 [17], replicated, may hold values from 0 to 63, as said below
- in_weight: bfloat16 [256, 84], replicated, may hold values from -0.625 to 0.625
- in_bias: float32 [256], replicated, may hold values from -4 to 4
- conv_weight: bfloat16 [2, 256, 2304], replicated, may hold values from -0.125 to 0.125
- cond_weight: bfloat16 [256, 1024], replicated, may hold values from -0.375 to 0.375
- out_weight: bfloat16 [84, 256], replicated, may hold values from -0.375 to 0.375
Outputs:
- advanced: float32 [16, 84, 128, 128], P('tm', None, 'lat')
Inputs may be any that keep to these rules, and one draw needn't show every extreme that they name: `step_levels`: strictly increasing; the first entry is 0 and the last is 63.
All inputs are finite; a program needn't handle non-finite values.
Results may differ from a plain program's by a relative error of at most 0.0055.
Values may be sent and summed in bfloat16 or wider, within the bound.
No kernel may reach another device: no remote copies, remote signals or barrier semaphores. Data moves between devices by JAX's collectives and lax.ppermute only.
A program may use at most 64 MiB of HBM per device.

v0:
```python
import jax
import jax.numpy as jnp
from jax import lax
from jax.sharding import PartitionSpec as P

LEVELS = 64
ITERS = 2
sigma_top = 1.0
sigma_low = 0.02
rho_power = 7.0


def extended(block, sides, width):
    for axis, dim in sides:
        count = lax.axis_size(axis)
        forward = [(i, i + 1) for i in range(count - 1)]
        backward = [(target, source) for source, target in forward]
        low = lax.ppermute(
            lax.slice_in_dim(block, block.shape[dim] - width, None, axis=dim), axis, forward
        )
        high = lax.ppermute(lax.slice_in_dim(block, 0, width, axis=dim), axis, backward)
        block = jnp.concatenate([low, block, high], axis=dim)
    return block


def carried_in(value, axis, join, neutral):
    count, mine = (lax.axis_size(axis), lax.axis_index(axis))
    pieces = lax.all_gather(value, axis)
    subtotal = jnp.full_like(value, 0) + jnp.asarray(neutral, value.dtype)

    def hop(position, subtotal):
        longer = join(subtotal, pieces[position])
        return jnp.where(position < mine, longer, subtotal)

    return lax.fori_loop(0, count - 1, hop, subtotal)


def from_root(array, axis, root):
    mine = lax.axis_index(axis) == root
    return lax.psum(jnp.where(mine, array, jnp.zeros_like(array)), axis)


def level_sigma(levels):
    fraction = levels.astype(jnp.float32) / (LEVELS - 1)
    root_value = sigma_top ** (1.0 / rho_power) + fraction * (
        sigma_low ** (1.0 / rho_power) - sigma_top ** (1.0 / rho_power)
    )
    return root_value**rho_power


def conditions_of(sigma_now, cond_weight):
    freq_count = cond_weight.shape[0] // 2
    frequency = 100.0 ** (jnp.arange(freq_count).astype(jnp.float32) / freq_count)
    phases = jnp.log(sigma_now) / 4.0 * frequency
    embedding = jnp.concatenate([jnp.cos(phases), jnp.sin(phases)]).astype(jnp.bfloat16)[None, :]
    conditions = jnp.dot(embedding, cond_weight, preferred_element_type=jnp.float32)[0]
    return jnp.split(conditions, 4)


def convolve(padded, weight):
    row_count = padded.shape[1] - 2
    shifted = []
    for offset_row in range(3):
        for offset_col in (-1, 0, 1):
            shifted.append(
                jnp.roll(padded[:, offset_row : offset_row + row_count, :], -offset_col, axis=2)
            )
    columns_all = jnp.concatenate(shifted, axis=0)
    flattened = columns_all.reshape(columns_all.shape[0], -1)
    response = jnp.dot(weight, flattened, preferred_element_type=jnp.float32)
    return response.reshape(weight.shape[0], row_count, padded.shape[2])


def project(scaled, in_weight, in_bias):
    channels, row_count, columns = scaled.shape
    hidden = (
        jnp.dot(in_weight, scaled.reshape(channels, -1), preferred_element_type=jnp.float32)
        + in_bias[:, None]
    )
    return hidden.reshape(-1, row_count, columns)


def field_drift(
    current, sigma_now, sigma_next, in_weight, in_bias, conv_weight, cond_weight, out_weight
):
    scale_one, shift_one, scale_two, shift_two = conditions_of(sigma_now, cond_weight)
    variance = sigma_now * sigma_now + 0.25
    scaled = (current / jnp.sqrt(variance)).astype(jnp.bfloat16)
    channels, row_count, columns = current.shape
    hidden_zero = project(scaled, in_weight, in_bias).astype(jnp.bfloat16)
    padded = extended(hidden_zero, (("lat", 1),), 1)
    response = convolve(padded, conv_weight[0])
    hidden_one = jax.nn.silu(
        response * (1.0 + scale_one[:, None, None]) + shift_one[:, None, None]
    ).astype(jnp.bfloat16)
    padded_one = extended(hidden_one, (("lat", 1),), 1)
    response = convolve(padded_one, conv_weight[1])
    hidden_two = hidden_one.astype(jnp.float32) + jax.nn.silu(
        response * (1.0 + scale_two[:, None, None]) + shift_two[:, None, None]
    )
    hidden_two = hidden_two.astype(jnp.bfloat16)
    network = jnp.dot(
        out_weight, hidden_two.reshape(hidden_two.shape[0], -1), preferred_element_type=jnp.float32
    )
    network = network.reshape(channels, row_count, columns)
    denoised = 0.25 / variance * current + 0.5 * sigma_now / jnp.sqrt(variance) * network
    return (current - denoised) * ((sigma_next - sigma_now) / sigma_now)


def add_pair(earlier_sum, later_sum):
    return earlier_sum + later_sum


def earlier_drifts(carried):
    return carried_in(carried, "tm", add_pair, jnp.zeros_like(carried))


def on_device(trajectory, step_levels, in_weight, in_bias, conv_weight, cond_weight, out_weight):
    time_slot = lax.axis_index("tm")
    current = trajectory[0]
    bounds = lax.dynamic_slice_in_dim(step_levels, time_slot, 2)
    sigmas = level_sigma(bounds)
    sigma_now = sigmas[0]
    sigma_next = sigmas[1]
    anchor = from_root(current, "tm", 0)
    result = current
    for sweep in range(ITERS):
        drift_term = field_drift(
            current, sigma_now, sigma_next, in_weight, in_bias, conv_weight, cond_weight, out_weight
        )
        earlier = earlier_drifts(drift_term)
        if sweep + 1 < ITERS:
            current = earlier + anchor
        else:
            result = earlier + anchor + drift_term
    return result[None]


def solution(mesh):
    in_specs = (P("tm", None, "lat", None), P(), P(), P(), P(), P(), P())
    out_specs = P("tm", None, "lat", None)
    return jax.shard_map(
        on_device, mesh=mesh, in_specs=in_specs, out_specs=out_specs, check_vma=False
    )
```

profile of v0, /device:TPU:1, one launch (start us, length us, event | category | flops | bytes accessed | tf_op | source)
XLA Modules:
  0.0 298.3 jit_solution(8111973741452247749)
XLA Ops:
  6.5 0.8 add_power_fusion
  7.3 0.6 fusion.115
  9.3 1.6 select_bitcast_fusion
  11.0 1.0 fusion.4
  12.1 4.0 %collective-permute-start = (bf16[256,1,128]{0,2,1:T(8,128)(2,1)S(1)}, bf16[256,1,128]{0,2,1:T(8,128)(2,1)S(1)}, u32[]{:S(2)}, u32[]{:S(2)}) collective-permute-start(bf16[256,1,128]{0,2,1:T(8,128)(2,1)S(1)} %get-tuple-element.258), channel_id=1, source_target_pairs={{0,1},{1,2},{2,3},{3,4},{4,5},{5,6},{6,7},{7,8},{8,9},{9,10},{10,1... | collective-permute-start | bytes 196616 | tf_op jit(solution)/shard_map/ppermute | solution.py:18
  16.1 1.3 collective-permute-start.1
  21.9 1.4 copy-done.8
  23.2 0.8 fusion.10
  24.2 4.0 %collective-permute-start.2 = (bf16[256,1,128]{0,2,1:T(8,128)(2,1)S(1)}, bf16[256,1,128]{0,2,1:T(8,128)(2,1)S(1)}, u32[]{:S(2)}, u32[]{:S(2)}) collective-permute-start(bf16[256,1,128]{0,2,1:T(8,128)(2,1)S(1)} %get-tuple-element.250), channel_id=1, source_target_pairs={{0,1},{1,2},{2,3},{3,4},{4,5},{5,6},{6,7},{7,8},{8,9},{9,10},{10,1... | collective-permute-start | bytes 196616 | tf_op jit(solution)/shard_map/ppermute | solution.py:18
  28.2 1.3 collective-permute-start.3
  29.5 3.7 %collective-permute-done.3 = bf16[256,1,128]{0,2,1:T(8,128)(2,1)S(1)} collective-permute-done((bf16[256,1,128]{0,2,1:T(8,128)(2,1)S(1)}, bf16[256,1,128]{0,2,1:T(8,128)(2,1)S(1)}, u32[]{:S(2)}, u32[]{:S(2)}) %collective-permute-start.3) | collective-permute-done | bytes 65568 | tf_op jit(solution)/shard_map/ppermute | solution.py:21
  34.0 1.4 copy-done.5
  35.4 3.2 %fusion.13 = f32[84,512]{1,0:T(8,128)S(1)} fusion(bf16[84,256]{1,0:T(8,128)(2,1)S(1)} %copy-done.10, bf16[2304,512]{0,1:T(8,128)(2,1)} %bitcast.145, bf16[2,256,2304]{2,1,0:T(8,128)(2,1)} %param.15, f32[512,256]{1,0:T(8,128)S(1)} %fusion.10, f32[256]{0:T(256)S(1)} %get-tuple-element.264, f32[256]{0:T(256)S(1)} %get-tuple-element.263, ...), kind=kOutput, calls=%fused_computation.21 | convolution fusion | flops 628140032 | bytes 4282372 | tf_op jit(solution)/shard_map/dot_general | solution.py:102
  38.7 0.7 subtract_multiply_fusion.1
  39.5 0.7 all-reduce.2.cloned.1.call-update
  40.3 51.2 %all-gather.4.cloned.1.call-done = f32[16,84,4,128]{3,2,1,0:T(4,128)} async-done(((f32[1,84,4,128]{3,2,1,0:T(4,128)}), f32[16,84,4,128]{3,2,1,0:T(4,128)}) %all-gather.4.cloned.1.call-update) | async-done | bytes 2752528 | tf_op jit(solution)/shard_map/all_gather | solution.py:28
  91.5 17.4 %while.28 = (s32[]{:T(128)}, f32[84,4,128]{2,1,0:T(4,128)S(1)}, s32[]{:T(128)}, f32[16,84,4,128]{3,2,1,0:T(4,128)}, s32[]{:T(128)}, /*index=5*/s32[]{:T(128)}) while((s32[]{:T(128)}, f32[84,4,128]{2,1,0:T(4,128)S(1)}, s32[]{:T(128)}, f32[16,84,4,128]{3,2,1,0:T(4,128)}, s32[]{:T(128)}, /*index=5*/s32[]{:T(128)}) %tuple.98), condition=%wide.region_1.2_spmd.clone, body=%wide.region_0.1_spmd.clone.sunk | while | flops 129028 | bytes 516189 | solution.py:35
  91.5 1.1 add_select_fusion.4
  92.7 1.1 add_select_fusion.4
  93.8 1.1 add_select_fusion.4
  95.0 1.1 add_select_fusion.4
  96.1 1.1 add_select_fusion.4
  97.3 1.1 add_select_fusion.4
  98.4 1.1 add_select_fusion.4
  99.6 1.1 add_select_fusion.4
  100.8 1.1 add_select_fusion.4
  101.9 1.1 add_select_fusion.4
  103.1 1.1 add_select_fusion.4
  104.2 1.1 add_select_fusion.4
  105.4 1.1 add_select_fusion.4
  106.5 1.1 add_select_fusion.4
  107.7 1.1 add_select_fusion.4
  108.9 92.6 %all-reduce.2.cloned.1.call-done = f32[84,4,128]{2,1,0:T(4,128)} async-done(((f32[84,4,128]{2,1,0:T(4,128)}), f32[84,4,128]{2,1,0:T(4,128)}) %all-reduce.2.cloned.1.call-update) | async-done | bytes 172048 | tf_op jit(solution)/shard_map/psum | solution.py:40
  201.5 1.0 divide_convert_fusion
  202.6 0.2 fusion.5
  202.8 3.1 %collective-permute-start.4 = (bf16[256,1,128]{0,2,1:T(8,128)(2,1)S(1)}, bf16[256,1,128]{0,2,1:T(8,128)(2,1)S(1)}, u32[]{:S(2)}, u32[]{:S(2)}) collective-permute-start(bf16[256,1,128]{0,2,1:T(8,128)(2,1)S(1)} %get-tuple-element.242), channel_id=1, source_target_pairs={{0,1},{1,2},{2,3},{3,4},{4,5},{5,6},{6,7},{7,8},{8,9},{9,10},{10,1... | collective-permute-start | bytes 196616 | tf_op jit(solution)/shard_map/ppermute | solution.py:18
  206.0 1.3 collective-permute-start.5
  207.5 3.8 %collective-permute-done.5 = bf16[256,1,128]{0,2,1:T(8,128)(2,1)S(1)} collective-permute-done((bf16[256,1,128]{0,2,1:T(8,128)(2,1)S(1)}, bf16[256,1,128]{0,2,1:T(8,128)(2,1)S(1)}, u32[]{:S(2)}, u32[]{:S(2)}) %collective-permute-start.5) | collective-permute-done | bytes 65568 | tf_op jit(solution)/shard_map/ppermute | solution.py:21
  212.0 1.4 copy-done.9
  213.4 0.8 fusion.8
  214.4 3.1 %collective-permute-start.6 = (bf16[256,1,128]{0,2,1:T(8,128)(2,1)S(1)}, bf16[256,1,128]{0,2,1:T(8,128)(2,1)S(1)}, u32[]{:S(2)}, u32[]{:S(2)}) collective-permute-start(bf16[256,1,128]{0,2,1:T(8,128)(2,1)S(1)} %get-tuple-element.234), channel_id=1, source_target_pairs={{0,1},{1,2},{2,3},{3,4},{4,5},{5,6},{6,7},{7,8},{8,9},{9,10},{10,1... | collective-permute-start | bytes 196616 | tf_op jit(solution)/shard_map/ppermute | solution.py:18
  217.5 1.3 collective-permute-start.7
  218.8 4.7 %collective-permute-done.7 = bf16[256,1,128]{0,2,1:T(8,128)(2,1)S(1)} collective-permute-done((bf16[256,1,128]{0,2,1:T(8,128)(2,1)S(1)}, bf16[256,1,128]{0,2,1:T(8,128)(2,1)S(1)}, u32[]{:S(2)}, u32[]{:S(2)}) %collective-permute-start.7) | collective-permute-done | bytes 65568 | tf_op jit(solution)/shard_map/ppermute | solution.py:21
  224.3 1.4 copy-done.6
  225.7 3.1 %fusion.12 = f32[84,512]{1,0:T(8,128)S(1)} fusion(bf16[84,256]{1,0:T(8,128)(2,1)S(1)} %copy-done.10, bf16[2304,512]{0,1:T(8,128)(2,1)} %bitcast.147, bf16[2,256,2304]{2,1,0:T(8,128)(2,1)} %param.15, f32[512,256]{1,0:T(8,128)S(1)} %fusion.8, f32[256]{0:T(256)S(1)} %get-tuple-element.264, f32[256]{0:T(256)S(1)} %get-tuple-element.263, ...), kind=kOutput, calls=%fused_computation.19 | convolution fusion | flops 628140032 | bytes 4282372 | tf_op jit(solution)/shard_map/dot_general | solution.py:102
  228.9 0.7 subtract_multiply_fusion
  229.6 44.0 %all-gather.6.cloned.1.call-done = f32[1344,4,128]{2,1,0:T(4,128)} async-done(((f32[84,4,128]{2,1,0:T(4,128)}), f32[1344,4,128]{2,1,0:T(4,128)}) %all-gather.6.cloned.1.call-update) | async-done | bytes 2752528 | tf_op jit(solution)/shard_map/all_gather | solution.py:28
  273.7 17.3 %while.29 = (s32[]{:T(128)}, f32[84,4,128]{2,1,0:T(4,128)S(1)}, s32[]{:T(128)}, f32[16,84,4,128]{3,2,1,0:T(4,128)}, s32[]{:T(128)}, /*index=5*/s32[]{:T(128)}) while((s32[]{:T(128)}, f32[84,4,128]{2,1,0:T(4,128)S(1)}, s32[]{:T(128)}, f32[16,84,4,128]{3,2,1,0:T(4,128)}, s32[]{:T(128)}, /*index=5*/s32[]{:T(128)}) %tuple.110), condition=%wide.region_4.5_spmd.clone, body=%wide.region_3.4_spmd.clone.sunk | while | flops 129028 | bytes 516189 | solution.py:35
  273.7 1.1 add_select_fusion.5
  274.8 1.1 add_select_fusion.5
  276.0 1.1 add_select_fusion.5
  277.1 1.1 add_select_fusion.5
  278.3 1.1 add_select_fusion.5
  279.4 1.1 add_select_fusion.5
  280.6 1.1 add_select_fusion.5
  281.8 1.1 add_select_fusion.5
  282.9 1.1 add_select_fusion.5
  284.1 1.1 add_select_fusion.5
  285.2 1.1 add_select_fusion.5
  286.4 1.1 add_select_fusion.5
  287.5 1.1 add_select_fusion.5
  288.7 1.1 add_select_fusion.5
  289.9 1.1 add_select_fusion.5
  291.0 0.7 add_bitcast_fusion
  (91 shorter events, 3.8 us)
Async XLA Ops:
  6.5 11.7 %copy-start = (bf16[256,1024]{1,0:T(8,128)(2,1)S(1)}, bf16[256,1024]{1,0:T(8,128)(2,1)}, u32[]{:S(2)}) copy-start(bf16[256,1024]{1,0:T(8,128)(2,1)} %param.16) | copy-start | bytes 1572868
  6.5 85.0 %all-gather.4.cloned.1.call-start = ((), (), s32[]{:S(2)}) async-start(), calls=%async_computation | async-start | bytes 2924544 | tf_op jit(solution)/shard_map/all_gather | solution.py:28
  12.1 9.1 %collective-permute-start = (bf16[256,1,128]{0,2,1:T(8,128)(2,1)S(1)}, bf16[256,1,128]{0,2,1:T(8,128)(2,1)S(1)}, u32[]{:S(2)}, u32[]{:S(2)}) collective-permute-start(bf16[256,1,128]{0,2,1:T(8,128)(2,1)S(1)} %get-tuple-element.258), channel_id=1, source_target_pairs={{0,1},{1,2},{2,3},{3,4},{4,5},{5,6},{6,7},{7,8},{8,9},{9,10},{10,1... | collective-permute-start | bytes 196616 | tf_op jit(solution)/shard_map/ppermute | solution.py:18
  16.1 5.1 %collective-permute-start.1 = (bf16[256,1,128]{0,2,1:T(8,128)(2,1)S(1)}, bf16[256,1,128]{0,2,1:T(8,128)(2,1)S(1)}, u32[]{:S(2)}, u32[]{:S(2)}) collective-permute-start(bf16[256,1,128]{0,2,1:T(8,128)(2,1)S(1)} %get-tuple-element.257), channel_id=1, source_target_pairs={{1,0},{2,1},{3,2},{4,3},{5,4},{6,5},{7,6},{8,7},{9,8},{10,9},{11,1... | collective-permute-start | bytes 196616 | tf_op jit(solution)/shard_map/ppermute | solution.py:21
  21.6 1.7 copy-start.8
  24.2 5.3 %collective-permute-start.2 = (bf16[256,1,128]{0,2,1:T(8,128)(2,1)S(1)}, bf16[256,1,128]{0,2,1:T(8,128)(2,1)S(1)}, u32[]{:S(2)}, u32[]{:S(2)}) collective-permute-start(bf16[256,1,128]{0,2,1:T(8,128)(2,1)S(1)} %get-tuple-element.250), channel_id=1, source_target_pairs={{0,1},{1,2},{2,3},{3,4},{4,5},{5,6},{6,7},{7,8},{8,9},{9,10},{10,1... | collective-permute-start | bytes 196616 | tf_op jit(solution)/shard_map/ppermute | solution.py:18
  28.2 5.0 %collective-permute-start.3 = (bf16[256,1,128]{0,2,1:T(8,128)(2,1)S(1)}, bf16[256,1,128]{0,2,1:T(8,128)(2,1)S(1)}, u32[]{:S(2)}, u32[]{:S(2)}) collective-permute-start(bf16[256,1,128]{0,2,1:T(8,128)(2,1)S(1)} %get-tuple-element.249), channel_id=1, source_target_pairs={{1,0},{2,1},{3,2},{4,3},{5,4},{6,5},{7,6},{8,7},{9,8},{10,9},{11,1... | collective-permute-start | bytes 196616 | tf_op jit(solution)/shard_map/ppermute | solution.py:21
  33.6 1.9 copy-start.10
  34.0 1.4 copy-start.5
  35.4 3.3 %copy-start.2 = (f32[1,84,4,128]{3,2,1,0:T(4,128)S(1)}, f32[1,84,4,128]{3,2,1,0:T(4,128)}, u32[]{:S(2)}) copy-start(f32[1,84,4,128]{3,2,1,0:T(4,128)} %param.11) | copy-start | bytes 516100
  38.7 163.9 %copy-start.4 = (bf16[256,84]{0,1:T(8,128)(2,1)S(1)}, bf16[256,84]{0,1:T(8,128)(2,1)}, u32[]{:S(2)}) copy-start(bf16[256,84]{0,1:T(8,128)(2,1)} %param.13) | copy-start | bytes 129028
  38.7 163.9 %copy-start.7 = (f32[256]{0:T(256)S(1)}, f32[256]{0:T(256)}, u32[]{:S(2)}) copy-start(f32[256]{0:T(256)} %param.14) | copy-start | bytes 3076
  39.4 162.1 %all-reduce.2.cloned.1.call-start = ((), (), s32[]{:S(2)}) async-start(), calls=%async_computation.1 | async-start | bytes 344064 | tf_op jit(solution)/shard_map/psum | solution.py:40
  40.2 233.5 %all-gather.6.cloned.1.call-start = ((), (), s32[]{:S(2)}) async-start(), calls=%async_computation.2 | async-start | bytes 2924544 | tf_op jit(solution)/shard_map/all_gather | solution.py:28
  202.8 4.7 %collective-permute-start.4 = (bf16[256,1,128]{0,2,1:T(8,128)(2,1)S(1)}, bf16[256,1,128]{0,2,1:T(8,128)(2,1)S(1)}, u32[]{:S(2)}, u32[]{:S(2)}) collective-permute-start(bf16[256,1,128]{0,2,1:T(8,128)(2,1)S(1)} %get-tuple-element.242), channel_id=1, source_target_pairs={{0,1},{1,2},{2,3},{3,4},{4,5},{5,6},{6,7},{7,8},{8,9},{9,10},{10,1... | collective-permute-start | bytes 196616 | tf_op jit(solution)/shard_map/ppermute | solution.py:18
  206.0 5.4 %collective-permute-start.5 = (bf16[256,1,128]{0,2,1:T(8,128)(2,1)S(1)}, bf16[256,1,128]{0,2,1:T(8,128)(2,1)S(1)}, u32[]{:S(2)}, u32[]{:S(2)}) collective-permute-start(bf16[256,1,128]{0,2,1:T(8,128)(2,1)S(1)} %get-tuple-element.241), channel_id=1, source_target_pairs={{1,0},{2,1},{3,2},{4,3},{5,4},{6,5},{7,6},{8,7},{9,8},{10,9},{11,1... | collective-permute-start | bytes 196616 | tf_op jit(solution)/shard_map/ppermute | solution.py:21
  211.7 1.7 copy-start.9
  214.4 4.5 %collective-permute-start.6 = (bf16[256,1,128]{0,2,1:T(8,128)(2,1)S(1)}, bf16[256,1,128]{0,2,1:T(8,128)(2,1)S(1)}, u32[]{:S(2)}, u32[]{:S(2)}) collective-permute-start(bf16[256,1,128]{0,2,1:T(8,128)(2,1)S(1)} %get-tuple-element.234), channel_id=1, source_target_pairs={{0,1},{1,2},{2,3},{3,4},{4,5},{5,6},{6,7},{7,8},{8,9},{9,10},{10,1... | collective-permute-start | bytes 196616 | tf_op jit(solution)/shard_map/ppermute | solution.py:18
  217.5 6.0 %collective-permute-start.7 = (bf16[256,1,128]{0,2,1:T(8,128)(2,1)S(1)}, bf16[256,1,128]{0,2,1:T(8,128)(2,1)S(1)}, u32[]{:S(2)}, u32[]{:S(2)}) collective-permute-start(bf16[256,1,128]{0,2,1:T(8,128)(2,1)S(1)} %get-tuple-element.233), channel_id=1, source_target_pairs={{1,0},{2,1},{3,2},{4,3},{5,4},{6,5},{7,6},{8,7},{9,8},{10,9},{11,1... | collective-permute-start | bytes 196616 | tf_op jit(solution)/shard_map/ppermute | solution.py:21
  224.3 1.4 copy-start.6
  228.8 62.2 %copy-start.3 = (f32[84,4,128]{2,1,0:T(4,128)S(1)}, f32[84,4,128]{2,1,0:T(4,128)}, u32[]{:S(2)}) copy-start(f32[84,4,128]{2,1,0:T(4,128)} %all-reduce.2.cloned.1.call-done) | copy-start | bytes 516100
  229.6 61.4 %copy-start.1 = (f32[42,8,128]{2,1,0:T(8,128)S(1)}, f32[42,8,128]{2,1,0:T(8,128)}, u32[]{:S(2)}) copy-start(f32[42,8,128]{2,1,0:T(8,128)} %subtract_multiply_fusion) | copy-start | bytes 516100
Sparse Core Ops, SparseCore 0:
  39.6 51.8 all-gather.3
  93.8 107.6 all-reduce.1
  229.7 43.8 all-gather.5
where the time goes:
time: 300 us; the launch traced here: 298 us
  waiting for transfers between devices  201 us (67%)
  other arithmetic  42.8 us (14%)
  starting transfers between devices  19.5 us (6%)
  between operations  18.7 us (6%)
  matrix products  9.37 us (3%)
  local copies, waits for them, and re-layouts  6.55 us (2%)
    all_gather x2, waiting for transfers between devices, carried_in(): pieces = lax.all_gather(value, axis)  95.3 us
    psum x1, waiting for transfers between devices, from_root(): return lax.psum(jnp.where(mine, array, jnp.zeros_like(array)), axis)  92.6 us
    select_n x30, other arithmetic, hop(): return jnp.where(position < mine, longer, subtotal)  34.4 us
    ppermute x4, starting transfers between devices, extended(): lax.ppermute(lax.slice_in_dim(block, block.shape[dim] - width, None, axis...  14.2 us
    ppermute x4, waiting for transfers between devices, extended(): lax.ppermute(lax.slice_in_dim(block, 0, width, axis=dim), axis, backward)  12.2 us
    dot_general x2, matrix products, field_drift(): jnp.dot(out_weight, hidden_two.reshape(hidden_two.shape[0], -1), preferre...  6.29 us
  transfers between devices with their start and end apart: 11, of which 7 were waited for; matrix products, arithmetic and copies ran while one was open for 6% of the time, Pallas kernels for 0%

commit v1 on v0

--- a/solution.py
+++ b/solution.py
@@ -8,6 +8,12 @@
 sigma_top = 1.0
 sigma_low = 0.02
 rho_power = 7.0
+
+
+def gather_and_add(x, axis):
+    blocks = lax.all_gather(x, axis, axis=0, tiled=False)
+    total = blocks.sum(axis=0)
+    return total
 
 
 def extended(block, sides, width):
@@ -37,7 +43,7 @@
 
 def from_root(array, axis, root):
     mine = lax.axis_index(axis) == root
-    return lax.psum(jnp.where(mine, array, jnp.zeros_like(array)), axis)
+    return gather_and_add(jnp.where(mine, array, jnp.zeros_like(array)), axis)
 
 
 def level_sigma(levels):

time: 300 us -> 226 us (0.75)
  waiting for transfers between devices: 201 us -> 127 us
    psum x1 -> x0, waiting for transfers between devices: 92.6 us -> none  [from_root(): return lax.psum(jnp.where(mine, array, jnp.zeros_like(array)), axis)]
    all_gather x0 -> x1, waiting for transfers between devices: none -> 29.2 us  [gather_and_add(): blocks = lax.all_gather(x, axis, axis=0, tiled=False)]
    all_gather x2, waiting for transfers between devices: 95.3 us -> 85.5 us  [carried_in(): pieces = lax.all_gather(value, axis)]
  transfers between devices with their start and end apart: 11 -> 11, of which waited for: 7 -> 6; matrix products, arithmetic and copies ran while one was open for 6% -> 4% of each run, Pallas kernels for 0% -> 0%
where the time goes in v1:
time: 226 us; the launch traced here: 225 us
  waiting for transfers between devices  127 us (56%)
  other arithmetic  44.1 us (20%)
  starting transfers between devices  19.6 us (9%)
  between operations  18.4 us (8%)
  matrix products  9.36 us (4%)
  local copies, waits for them, and re-layouts  6.57 us (3%)
    all_gather x2, waiting for transfers between devices, carried_in(): pieces = lax.all_gather(value, axis)  85.5 us
    select_n x30, other arithmetic, hop(): return jnp.where(position < mine, longer, subtotal)  34.4 us
    all_gather x1, waiting for transfers between devices, gather_and_add(): blocks = lax.all_gather(x, axis, axis=0, tiled=False)  29.2 us
    ppermute x4, starting transfers between devices, extended(): lax.ppermute(lax.slice_in_dim(block, block.shape[dim] - width, None, axis...  14.4 us
    ppermute x4, waiting for transfers between devices, extended(): lax.ppermute(lax.slice_in_dim(block, 0, width, axis=dim), axis, backward)  11.8 us
    dot_general x2, matrix products, field_drift(): jnp.dot(out_weight, hidden_two.reshape(hidden_two.shape[0], -1), preferre...  6.29 us
    unnamed x26, local copies, waits for them, and re-layouts  5.75 us
    ppermute x4, starting transfers between devices, extended(): lax.ppermute(lax.slice_in_dim(block, 0, width, axis=dim), axis, backward)  5.17 us
  transfers between devices with their start and end apart: 11, of which 6 were waited for; matrix products, arithmetic and copies ran while one was open for 4% of the time, Pallas kernels for 0%

profile of v1, /device:TPU:1, one launch (start us, length us, event | category | flops | bytes accessed | tf_op | source)
XLA Modules:
  0.0 225.0 jit_solution(14181750596278524803)
XLA Ops:
  6.5 0.8 add_power_fusion
  7.3 0.6 fusion.115
  9.3 1.6 broadcast_select_fusion
  11.0 1.0 fusion.4
  12.0 4.0 %collective-permute-start = (bf16[256,1,128]{0,2,1:T(8,128)(2,1)S(1)}, bf16[256,1,128]{0,2,1:T(8,128)(2,1)S(1)}, u32[]{:S(2)}, u32[]{:S(2)}) collective-permute-start(bf16[256,1,128]{0,2,1:T(8,128)(2,1)S(1)} %get-tuple-element.258), channel_id=1, source_target_pairs={{0,1},{1,2},{2,3},{3,4},{4,5},{5,6},{6,7},{7,8},{8,9},{9,10},{10,1... | collective-permute-start | bytes 196616 | tf_op jit(solution)/shard_map/ppermute | solution.py:24
  16.1 1.3 collective-permute-start.1
  21.1 0.2 fusion.54
  21.7 1.4 copy-done.7
  23.1 0.8 fusion.10
  24.1 4.0 %collective-permute-start.2 = (bf16[256,1,128]{0,2,1:T(8,128)(2,1)S(1)}, bf16[256,1,128]{0,2,1:T(8,128)(2,1)S(1)}, u32[]{:S(2)}, u32[]{:S(2)}) collective-permute-start(bf16[256,1,128]{0,2,1:T(8,128)(2,1)S(1)} %get-tuple-element.250), channel_id=1, source_target_pairs={{0,1},{1,2},{2,3},{3,4},{4,5},{5,6},{6,7},{7,8},{8,9},{9,10},{10,1... | collective-permute-start | bytes 196616 | tf_op jit(solution)/shard_map/ppermute | solution.py:24
  28.1 1.3 collective-permute-start.3
  29.4 3.8 %collective-permute-done.3 = bf16[256,1,128]{0,2,1:T(8,128)(2,1)S(1)} collective-permute-done((bf16[256,1,128]{0,2,1:T(8,128)(2,1)S(1)}, bf16[256,1,128]{0,2,1:T(8,128)(2,1)S(1)}, u32[]{:S(2)}, u32[]{:S(2)}) %collective-permute-start.3) | collective-permute-done | bytes 65568 | tf_op jit(solution)/shard_map/ppermute | solution.py:27
  34.0 1.4 copy-done.4
  35.4 3.2 %fusion.13 = f32[84,512]{1,0:T(8,128)S(1)} fusion(bf16[84,256]{1,0:T(8,128)(2,1)S(1)} %copy-done.9, bf16[2304,512]{0,1:T(8,128)(2,1)} %bitcast.143, bf16[2,256,2304]{2,1,0:T(8,128)(2,1)} %param.15, f32[512,256]{1,0:T(8,128)S(1)} %fusion.10, f32[256]{0:T(256)S(1)} %get-tuple-element.264, f32[256]{0:T(256)S(1)} %get-tuple-element.263, ...), kind=kOutput, calls=%fused_computation.21 | convolution fusion | flops 628140032 | bytes 4282372 | tf_op jit(solution)/shard_map/dot_general | solution.py:108
  38.6 0.7 subtract_multiply_fusion.1
  39.4 29.2 %all-gather.7.cloned.1.call-done = f32[16,84,4,128]{3,2,1,0:T(4,128)} async-done(((f32[1,84,4,128]{3,2,1,0:T(4,128)}), f32[16,84,4,128]{3,2,1,0:T(4,128)}) %all-gather.7.cloned.1.call-update) | async-done | bytes 2752528 | tf_op jit(solution)/shard_map/all_gather | solution.py:14
  68.6 2.2 reduce_sum.9
  70.8 41.6 %all-gather.5.cloned.1.call-done = f32[16,84,4,128]{3,2,1,0:T(4,128)} async-done(((f32[1,84,4,128]{3,2,1,0:T(4,128)}), f32[16,84,4,128]{3,2,1,0:T(4,128)}) %all-gather.5.cloned.1.call-update) | async-done | bytes 2752528 | tf_op jit(solution)/shard_map/all_gather | solution.py:34
  112.5 17.3 %while.28 = (s32[]{:T(128)}, f32[84,4,128]{2,1,0:T(4,128)S(1)}, s32[]{:T(128)}, f32[16,84,4,128]{3,2,1,0:T(4,128)}, s32[]{:T(128)}, /*index=5*/s32[]{:T(128)}) while((s32[]{:T(128)}, f32[84,4,128]{2,1,0:T(4,128)S(1)}, s32[]{:T(128)}, f32[16,84,4,128]{3,2,1,0:T(4,128)}, s32[]{:T(128)}, /*index=5*/s32[]{:T(128)}) %tuple.98), condition=%wide.region_1.2_spmd.clone, body=%wide.region_0.1_spmd.clone.sunk | while | flops 129028 | bytes 516189 | solution.py:41
  112.5 1.1 add_select_fusion.4
  113.6 1.1 add_select_fusion.4
  114.8 1.1 add_select_fusion.4
  115.9 1.1 add_select_fusion.4
  117.1 1.1 add_select_fusion.4
  118.2 1.1 add_select_fusion.4
  119.4 1.1 add_select_fusion.4
  120.6 1.1 add_select_fusion.4
  121.7 1.1 add_select_fusion.4
  122.9 1.1 add_select_fusion.4
  124.0 1.1 add_select_fusion.4
  125.2 1.1 add_select_fusion.4
  126.3 1.1 add_select_fusion.4
  127.5 1.1 add_select_fusion.4
  128.7 1.1 add_select_fusion.4
  130.0 0.2 fusion.5
  130.2 3.2 %collective-permute-start.4 = (bf16[256,1,128]{0,2,1:T(8,128)(2,1)S(1)}, bf16[256,1,128]{0,2,1:T(8,128)(2,1)S(1)}, u32[]{:S(2)}, u32[]{:S(2)}) collective-permute-start(bf16[256,1,128]{0,2,1:T(8,128)(2,1)S(1)} %get-tuple-element.242), channel_id=1, source_target_pairs={{0,1},{1,2},{2,3},{3,4},{4,5},{5,6},{6,7},{7,8},{8,9},{9,10},{10,1... | collective-permute-start | bytes 196616 | tf_op jit(solution)/shard_map/ppermute | solution.py:24
  133.5 1.3 collective-permute-start.5
  134.8 3.7 %collective-permute-done.5 = bf16[256,1,128]{0,2,1:T(8,128)(2,1)S(1)} collective-permute-done((bf16[256,1,128]{0,2,1:T(8,128)(2,1)S(1)}, bf16[256,1,128]{0,2,1:T(8,128)(2,1)S(1)}, u32[]{:S(2)}, u32[]{:S(2)}) %collective-permute-start.5) | collective-permute-done | bytes 65568 | tf_op jit(solution)/shard_map/ppermute | solution.py:27
  139.1 1.4 copy-done.8
  140.5 0.8 fusion.8
  141.5 3.1 %collective-permute-start.6 = (bf16[256,1,128]{0,2,1:T(8,128)(2,1)S(1)}, bf16[256,1,128]{0,2,1:T(8,128)(2,1)S(1)}, u32[]{:S(2)}, u32[]{:S(2)}) collective-permute-start(bf16[256,1,128]{0,2,1:T(8,128)(2,1)S(1)} %get-tuple-element.234), channel_id=1, source_target_pairs={{0,1},{1,2},{2,3},{3,4},{4,5},{5,6},{6,7},{7,8},{8,9},{9,10},{10,1... | collective-permute-start | bytes 196616 | tf_op jit(solution)/shard_map/ppermute | solution.py:24
  144.6 1.3 collective-permute-start.7
  145.9 4.4 %collective-permute-done.7 = bf16[256,1,128]{0,2,1:T(8,128)(2,1)S(1)} collective-permute-done((bf16[256,1,128]{0,2,1:T(8,128)(2,1)S(1)}, bf16[256,1,128]{0,2,1:T(8,128)(2,1)S(1)}, u32[]{:S(2)}, u32[]{:S(2)}) %collective-permute-start.7) | collective-permute-done | bytes 65568 | tf_op jit(solution)/shard_map/ppermute | solution.py:27
  151.1 1.4 copy-done.5
  152.5 3.1 %fusion.12 = f32[84,512]{1,0:T(8,128)S(1)} fusion(bf16[84,256]{1,0:T(8,128)(2,1)S(1)} %copy-done.9, bf16[2304,512]{0,1:T(8,128)(2,1)} %bitcast.145, bf16[2,256,2304]{2,1,0:T(8,128)(2,1)} %param.15, f32[512,256]{1,0:T(8,128)S(1)} %fusion.8, f32[256]{0:T(256)S(1)} %get-tuple-element.264, f32[256]{0:T(256)S(1)} %get-tuple-element.263, ...), kind=kOutput, calls=%fused_computation.19 | convolution fusion | flops 628140032 | bytes 4282372 | tf_op jit(solution)/shard_map/dot_general | solution.py:108
  155.7 0.7 subtract_multiply_fusion
  156.5 43.9 %all-gather.9.cloned.1.call-done = f32[1344,4,128]{2,1,0:T(4,128)} async-done(((f32[84,4,128]{2,1,0:T(4,128)}), f32[1344,4,128]{2,1,0:T(4,128)}) %all-gather.9.cloned.1.call-update) | async-done | bytes 2752528 | tf_op jit(solution)/shard_map/all_gather | solution.py:34
  200.3 17.3 %while.29 = (s32[]{:T(128)}, f32[84,4,128]{2,1,0:T(4,128)S(1)}, s32[]{:T(128)}, f32[16,84,4,128]{3,2,1,0:T(4,128)}, s32[]{:T(128)}, /*index=5*/s32[]{:T(128)}) while((s32[]{:T(128)}, f32[84,4,128]{2,1,0:T(4,128)S(1)}, s32[]{:T(128)}, f32[16,84,4,128]{3,2,1,0:T(4,128)}, s32[]{:T(128)}, /*index=5*/s32[]{:T(128)}) %tuple.110), condition=%wide.region_4.5_spmd.clone, body=%wide.region_3.4_spmd.clone.sunk | while | flops 129028 | bytes 516189 | solution.py:41
  200.3 1.1 add_select_fusion.5
  201.5 1.1 add_select_fusion.5
  202.7 1.1 add_select_fusion.5
  203.8 1.1 add_select_fusion.5
  205.0 1.1 add_select_fusion.5
  206.1 1.1 add_select_fusion.5
  207.3 1.1 add_select_fusion.5
  208.4 1.1 add_select_fusion.5
  209.6 1.1 add_select_fusion.5
  210.8 1.1 add_select_fusion.5
  211.9 1.1 add_select_fusion.5
  213.1 1.1 add_select_fusion.5
  214.2 1.1 add_select_fusion.5
  215.4 1.1 add_select_fusion.5
  216.5 1.1 add_select_fusion.5
  217.7 0.7 add_bitcast_fusion
  (90 shorter events, 3.4 us)
Async XLA Ops:
  6.5 11.7 %copy-start = (bf16[256,1024]{1,0:T(8,128)(2,1)S(1)}, bf16[256,1024]{1,0:T(8,128)(2,1)}, u32[]{:S(2)}) copy-start(bf16[256,1024]{1,0:T(8,128)(2,1)} %param.16) | copy-start | bytes 1572868
  6.5 62.1 %all-gather.7.cloned.1.call-start = ((), (), s32[]{:S(2)}) async-start(), calls=%async_computation.1 | async-start | bytes 2924544 | tf_op jit(solution)/shard_map/all_gather | solution.py:14
  12.0 9.0 %collective-permute-start = (bf16[256,1,128]{0,2,1:T(8,128)(2,1)S(1)}, bf16[256,1,128]{0,2,1:T(8,128)(2,1)S(1)}, u32[]{:S(2)}, u32[]{:S(2)}) collective-permute-start(bf16[256,1,128]{0,2,1:T(8,128)(2,1)S(1)} %get-tuple-element.258), channel_id=1, source_target_pairs={{0,1},{1,2},{2,3},{3,4},{4,5},{5,6},{6,7},{7,8},{8,9},{9,10},{10,1... | collective-permute-start | bytes 196616 | tf_op jit(solution)/shard_map/ppermute | solution.py:24
  16.1 5.0 %collective-permute-start.1 = (bf16[256,1,128]{0,2,1:T(8,128)(2,1)S(1)}, bf16[256,1,128]{0,2,1:T(8,128)(2,1)S(1)}, u32[]{:S(2)}, u32[]{:S(2)}) collective-permute-start(bf16[256,1,128]{0,2,1:T(8,128)(2,1)S(1)} %get-tuple-element.257), channel_id=1, source_target_pairs={{1,0},{2,1},{3,2},{4,3},{5,4},{6,5},{7,6},{8,7},{9,8},{10,9},{11,1... | collective-permute-start | bytes 196616 | tf_op jit(solution)/shard_map/ppermute | solution.py:27
  17.4 95.1 %all-gather.5.cloned.1.call-start = ((), (), s32[]{:S(2)}) async-start(), calls=%async_computation | async-start | bytes 2924544 | tf_op jit(solution)/shard_map/all_gather | solution.py:34
  21.4 1.7 copy-start.7
  24.1 5.3 %collective-permute-start.2 = (bf16[256,1,128]{0,2,1:T(8,128)(2,1)S(1)}, bf16[256,1,128]{0,2,1:T(8,128)(2,1)S(1)}, u32[]{:S(2)}, u32[]{:S(2)}) collective-permute-start(bf16[256,1,128]{0,2,1:T(8,128)(2,1)S(1)} %get-tuple-element.250), channel_id=1, source_target_pairs={{0,1},{1,2},{2,3},{3,4},{4,5},{5,6},{6,7},{7,8},{8,9},{9,10},{10,1... | collective-permute-start | bytes 196616 | tf_op jit(solution)/shard_map/ppermute | solution.py:24
  28.1 5.1 %collective-permute-start.3 = (bf16[256,1,128]{0,2,1:T(8,128)(2,1)S(1)}, bf16[256,1,128]{0,2,1:T(8,128)(2,1)S(1)}, u32[]{:S(2)}, u32[]{:S(2)}) collective-permute-start(bf16[256,1,128]{0,2,1:T(8,128)(2,1)S(1)} %get-tuple-element.249), channel_id=1, source_target_pairs={{1,0},{2,1},{3,2},{4,3},{5,4},{6,5},{7,6},{8,7},{9,8},{10,9},{11,1... | collective-permute-start | bytes 196616 | tf_op jit(solution)/shard_map/ppermute | solution.py:27
  33.5 1.9 copy-start.9
  34.0 1.4 copy-start.4
  35.4 3.2 %copy-start.2 = (f32[1,84,4,128]{3,2,1,0:T(4,128)S(1)}, f32[1,84,4,128]{3,2,1,0:T(4,128)}, u32[]{:S(2)}) copy-start(f32[1,84,4,128]{3,2,1,0:T(4,128)} %param.11) | copy-start | bytes 516100
  39.4 161.0 %all-gather.9.cloned.1.call-start = ((), (), s32[]{:S(2)}) async-start(), calls=%async_computation.2 | async-start | bytes 2924544 | tf_op jit(solution)/shard_map/all_gather | solution.py:34
  70.8 59.1 %copy-start.3 = (bf16[256,84]{0,1:T(8,128)(2,1)S(1)}, bf16[256,84]{0,1:T(8,128)(2,1)}, u32[]{:S(2)}) copy-start(bf16[256,84]{0,1:T(8,128)(2,1)} %param.13) | copy-start | bytes 129028
  70.8 59.1 %copy-start.6 = (f32[256]{0:T(256)S(1)}, f32[256]{0:T(256)}, u32[]{:S(2)}) copy-start(f32[256]{0:T(256)} %param.14) | copy-start | bytes 3076
  130.2 4.6 %collective-permute-start.4 = (bf16[256,1,128]{0,2,1:T(8,128)(2,1)S(1)}, bf16[256,1,128]{0,2,1:T(8,128)(2,1)S(1)}, u32[]{:S(2)}, u32[]{:S(2)}) collective-permute-start(bf16[256,1,128]{0,2,1:T(8,128)(2,1)S(1)} %get-tuple-element.242), channel_id=1, source_target_pairs={{0,1},{1,2},{2,3},{3,4},{4,5},{5,6},{6,7},{7,8},{8,9},{9,10},{10,1... | collective-permute-start | bytes 196616 | tf_op jit(solution)/shard_map/ppermute | solution.py:24
  133.5 5.0 %collective-permute-start.5 = (bf16[256,1,128]{0,2,1:T(8,128)(2,1)S(1)}, bf16[256,1,128]{0,2,1:T(8,128)(2,1)S(1)}, u32[]{:S(2)}, u32[]{:S(2)}) collective-permute-start(bf16[256,1,128]{0,2,1:T(8,128)(2,1)S(1)} %get-tuple-element.241), channel_id=1, source_target_pairs={{1,0},{2,1},{3,2},{4,3},{5,4},{6,5},{7,6},{8,7},{9,8},{10,9},{11,1... | collective-permute-start | bytes 196616 | tf_op jit(solution)/shard_map/ppermute | solution.py:27
  138.8 1.7 copy-start.8
  141.5 4.4 %collective-permute-start.6 = (bf16[256,1,128]{0,2,1:T(8,128)(2,1)S(1)}, bf16[256,1,128]{0,2,1:T(8,128)(2,1)S(1)}, u32[]{:S(2)}, u32[]{:S(2)}) collective-permute-start(bf16[256,1,128]{0,2,1:T(8,128)(2,1)S(1)} %get-tuple-element.234), channel_id=1, source_target_pairs={{0,1},{1,2},{2,3},{3,4},{4,5},{5,6},{6,7},{7,8},{8,9},{9,10},{10,1... | collective-permute-start | bytes 196616 | tf_op jit(solution)/shard_map/ppermute | solution.py:24
  144.6 5.7 %collective-permute-start.7 = (bf16[256,1,128]{0,2,1:T(8,128)(2,1)S(1)}, bf16[256,1,128]{0,2,1:T(8,128)(2,1)S(1)}, u32[]{:S(2)}, u32[]{:S(2)}) collective-permute-start(bf16[256,1,128]{0,2,1:T(8,128)(2,1)S(1)} %get-tuple-element.233), channel_id=1, source_target_pairs={{1,0},{2,1},{3,2},{4,3},{5,4},{6,5},{7,6},{8,7},{9,8},{10,9},{11,1... | collective-permute-start | bytes 196616 | tf_op jit(solution)/shard_map/ppermute | solution.py:27
  151.1 1.4 copy-start.5
  156.4 61.3 %copy-start.1 = (f32[42,8,128]{2,1,0:T(8,128)S(1)}, f32[42,8,128]{2,1,0:T(8,128)}, u32[]{:S(2)}) copy-start(f32[42,8,128]{2,1,0:T(8,128)} %subtract_multiply_fusion) | copy-start | bytes 516100
Sparse Core Ops, SparseCore 0:
  17.5 51.0 all-gather.6
  70.7 41.6 all-gather.4
  156.6 43.7 all-gather.8
